TPU v7x, 128 devices: a whole 4x4x4 slice. The times are simulated.
128 devices in a mesh: scen: 8 (over x, z_hi), border: 16 (over y, z_lo, core).
Axes of the slice: x: 4, y: 4, z: 4 (z_hi: 2, z_lo: 2; z = z_hi * 2 + z_lo), core: 2. Of those that a mesh axis runs over, the one named last changes fastest.
Arguments:
- border: bfloat16 [16, 512, 65536], P('scen', None, 'border'), may hold values from -1.5 to 1.5
- blocks: float32 [16, 512, 512], P('scen'), may hold values from -60 to 64, as said below
- root_diag: float32 [65536], P('border'), may hold values from 4 to 128
- live_rows: int32 [16], P('scen'), may hold values from 128 to 512, as said below
- panel_ids: int32 [4], replicated, may hold values from 0 to 255
Outputs:
- root_rows: float32 [16, 4096, 1024], P('border', 'scen')
- factor: float32 [4, 256, 256], replicated
Inputs may be any that keep to these rules, and one draw needn't show every extreme that they name: blocks[i] is a Gram matrix plus a positive diagonal of at least 1, hence symmetric positive definite. `live_rows`: each entry is a multiple of 128, and some scenario has 512.
All inputs are finite; a program needn't handle non-finite values.
Results may differ from a plain program's by a relative error of at most 0.0017.
Values may be sent and summed in bfloat16 or wider, within the bound.
No kernel may reach another device: no remote copies, remote signals or barrier semaphores. Data moves between devices by JAX's collectives and lax.ppermute only.
A program may use at most 128 MiB of HBM per device.

v0:
```python
import jax
import jax.numpy as jnp
from jax import lax
from jax.sharding import PartitionSpec as P

PW = 256
PANELS = 4


def broadcast(value, axis, source):
    kept = jnp.where(lax.axis_index(axis) == source, value, 0).astype(value.dtype)
    return lax.psum(kept, axis)


def on_device(border, blocks, root_diag, live_rows, panel_ids):
    scen_local, order, width = border.shape
    scen_count = lax.axis_size("scen")
    share = width // scen_count
    border_pos = lax.axis_index("border")
    scen_pos = lax.axis_index("scen")
    slabs = width // PW
    levels = jnp.arange(order, dtype=jnp.int32)
    keep = levels[None, :, None] >= (order - live_rows)[:, None, None]
    masked = jnp.where(keep, border, jnp.zeros_like(border))
    lower_factor = jnp.linalg.cholesky(blocks)
    identity = jnp.broadcast_to(jnp.eye(order, dtype=jnp.float32), blocks.shape)
    inverse = lax.linalg.triangular_solve(
        lower_factor, identity, left_side=True, lower=True
    ).astype(jnp.bfloat16)
    solved = jnp.einsum("ikr,irc->ikc", inverse, masked, preferred_element_type=jnp.float32).astype(
        jnp.bfloat16
    )
    panel_list = []
    for position in range(PANELS):
        chosen = panel_ids[position]
        owner = chosen // slabs
        offset = chosen % slabs * PW
        own_cols = lax.dynamic_slice_in_dim(solved, offset, PW, 2)
        panel_cols = broadcast(own_cols, "border", owner)
        panel_list.append(panel_cols)
    panels = jnp.concatenate(panel_list, axis=2)
    schur_cols = lax.psum_scatter(
        lax.dot_general(
            solved, panels, (((0, 1), (0, 1)), ((), ())), preferred_element_type=jnp.float32
        ),
        "scen",
        scatter_dimension=0,
        tiled=True,
    )
    base = border_pos * width + scen_pos * share
    global_cols = base + jnp.arange(share, dtype=jnp.int32)
    window_cols = (panel_ids[:, None] * PW + jnp.arange(PW, dtype=jnp.int32)[None, :]).reshape(-1)
    diag_part = lax.dynamic_slice_in_dim(root_diag, scen_pos * share, share)
    matches = global_cols[:, None] == window_cols[None, :]
    schur_cols = schur_cols + jnp.where(matches, diag_part[:, None], jnp.zeros((), jnp.float32))
    tiles = []
    for position in range(PANELS):
        local_start = panel_ids[position] * PW - base
        holds = (local_start >= 0) & (local_start < share)
        safe_start = jnp.clip(local_start, 0, share - PW)
        tile = lax.dynamic_slice(schur_cols, (safe_start, jnp.int32(position * PW)), (PW, PW))
        tiles.append(jnp.where(holds, tile, jnp.zeros_like(tile)))
    diag_block = lax.psum(jnp.stack(tiles), ("scen", "border"))
    factor = jnp.linalg.cholesky(diag_block)
    eye_stack = jnp.broadcast_to(jnp.eye(PW, dtype=jnp.float32), diag_block.shape)
    factor_inverse = lax.linalg.triangular_solve(factor, eye_stack, left_side=True, lower=True)
    shaped = schur_cols.reshape(share, PANELS, PW)
    solved_rows = jnp.einsum(
        "cpj,pkj->cpk", shaped, factor_inverse, precision=lax.Precision.HIGHEST
    )
    return (solved_rows.reshape(1, share, PANELS * PW), factor)


def solution(mesh):
    placed = (P("scen", None, "border"), P("scen", None, None), P("border"), P("scen"), P())
    return jax.shard_map(
        on_device,
        mesh=mesh,
        in_specs=placed,
        out_specs=(P("border", "scen", None), P()),
        check_vma=False,
    )
```

profile of v0, /device:TPU:1, one launch (start us, length us, event | category | flops | bytes accessed | tf_op | source)
XLA Modules:
  0.0 1063.2 jit_solution(11236807815509924732)
XLA Ops:
  20.5 3.0 copy.27
  27.0 23.5 %custom-call.50 = f32[2,128,128]{2,1,0:T(8,128)S(1)} custom-call(f32[2,128,128]{2,1,0:T(8,128)S(1)} %cholesky.390), custom_call_target="Cholesky" | custom-call | tf_op jit(solution)/shard_map/jit(cholesky)/cholesky | solution.py:25
  50.5 19.7 %custom-call.51 = f32[2,1,128,128]{2,3,1,0:T(8,128)S(1)} custom-call(f32[2,1,128,128]{3,2,1,0:T(8,128)S(1)} %select_bitcast_fusion.7), custom_call_target="InvertDiagBlocksLowerTriangular" | custom-call | tf_op jit(solution)/shard_map/jit(cholesky)/cholesky | solution.py:25
  74.1 24.9 %custom-call.52 = f32[2,128,128]{2,1,0:T(8,128)} custom-call(f32[2,128,128]{2,1,0:T(8,128)} %cholesky.394), custom_call_target="Cholesky" | custom-call | tf_op jit(solution)/shard_map/jit(cholesky)/cholesky | solution.py:25
  100.6 21.3 %custom-call.53 = f32[2,1,128,128]{2,3,1,0:T(8,128)} custom-call(f32[2,1,128,128]{3,2,1,0:T(8,128)} %get-tuple-element.72), custom_call_target="InvertDiagBlocksLowerTriangular" | custom-call | tf_op jit(solution)/shard_map/jit(cholesky)/cholesky | solution.py:25
  125.4 24.9 %custom-call.54 = f32[2,128,128]{2,1,0:T(8,128)} custom-call(f32[2,128,128]{2,1,0:T(8,128)} %cholesky.399), custom_call_target="Cholesky" | custom-call | tf_op jit(solution)/shard_map/jit(cholesky)/cholesky | solution.py:25
  151.9 21.1 %custom-call.55 = f32[2,1,128,128]{2,3,1,0:T(8,128)} custom-call(f32[2,1,128,128]{3,2,1,0:T(8,128)} %get-tuple-element.70), custom_call_target="InvertDiagBlocksLowerTriangular" | custom-call | tf_op jit(solution)/shard_map/jit(cholesky)/cholesky | solution.py:25
  175.7 23.9 %custom-call.56 = f32[2,128,128]{2,1,0:T(8,128)S(1)} custom-call(f32[2,128,128]{2,1,0:T(8,128)S(1)} %convolution_subtract_fusion.6), custom_call_target="Cholesky" | custom-call | tf_op jit(solution)/shard_map/jit(cholesky)/cholesky | solution.py:25
  203.6 14.1 %while.2 = (s32[]{:T(128)}, f32[2,512,512]{2,1,0:T(8,128)}, s32[4,2]{0,1:T(2,128)S(1)}, f32[4,2,128,128]{3,2,0,1:T(8,128)}, s32[]{:T(128)}) while((s32[]{:T(128)}, f32[2,512,512]{2,1,0:T(8,128)}, s32[4,2]{0,1:T(2,128)S(1)}, f32[4,2,128,128]{3,2,0,1:T(8,128)}, s32[]{:T(128)}) %tuple.68), condition=%wide.while_cond, body=%wide.while_body.sunk | while | flops 2 | bytes 263777 | solution.py:27
  204.2 2.9 bitcast_dynamic-update-slice_fusion.4
  207.8 2.9 bitcast_dynamic-update-slice_fusion.4
  217.7 79.4 %custom-call.57 = f32[2,4,128,128]{2,3,1,0:T(8,128)S(1)} custom-call(f32[2,4,128,128]{3,2,1,0:T(8,128)} %bitcast.125), custom_call_target="InvertDiagBlocksLowerTriangular" | custom-call | tf_op jit(solution)/shard_map/triangular_solve | solution.py:27
  305.3 11.2 %fusion.3 = bf16[2,512,4096]{2,1,0:T(8,128)(2,1)} fusion(bf16[2,512,4096]{2,1,0:T(8,128)(2,1)} %param.5, pred[2,512]{1,0:T(4,128)(4,1)S(1)} %iota_compare_fusion.6, bf16[2,128,512]{2,1,0:T(8,128)(2,1)S(1)} %convolution_convert_fusion, bf16[2,128,512]{2,1,0:T(8,128)(2,1)S(1)} %get-tuple-element.80, bf16[2,128,512]{2,1,0:T(8,128)(2,1)S(1)} %get-tuple-element.82, ...), kind=kOutput, calls=%fused_computation.8 | convolution fusion | flops 4307550208 | bytes 17826816 | tf_op jit(solution)/shard_map/ikr,irc->ikc/dot_general | solution.py:30
  316.5 3.0 dynamic-slice_select_fusion.3
  319.6 127.5 %all-reduce.8.cloned.1.call-done = (bf16[2,512,256]{2,1,0:T(8,128)(2,1)}, bf16[2,512,256]{2,1,0:T(8,128)(2,1)}, bf16[2,512,256]{2,1,0:T(8,128)(2,1)}, bf16[2,512,256]{2,1,0:T(8,128)(2,1)}) async-done(((bf16[2,512,256]{2,1,0:T(8,128)(2,1)}, bf16[2,512,256]{2,1,0:T(8,128)(2,1)}, bf16[2,512,256]{2,1,0:T(8,128)(2,1)}, bf16[2,512,256]{2,1,0:T(8,128)(2,1)}), (bf16[2,512,256]{2,1,0:T(8,128)(2,1)}, ...) | async-done | bytes 2097168 | tf_op jit(solution)/shard_map/psum | solution.py:12
  447.1 15.2 %convolution_bitcast_fusion = f32[4096,1024]{0,1:T(8,128)} fusion(bf16[2,512,4096]{2,1,0:T(8,128)(2,1)} %fusion.3, bf16[2,512,256]{2,1,0:T(8,128)(2,1)} %get-tuple-element.44, bf16[2,512,256]{2,1,0:T(8,128)(2,1)} %get-tuple-element.45, bf16[2,512,256]{2,1,0:T(8,128)(2,1)} %get-tuple-element.46, bf16[2,512,256]{2,1,0:T(8,128)(2,1)} %get-tuple-element.47), kind=kOutput, calls=%fused_computation.4 | convolution fusion | flops 8598323200 | bytes 27262976 | tf_op jit(solution)/shard_map/dot_general | solution.py:43
  465.7 189.8 %reduce-scatter.2.cloned.1.call-done = f32[512,1024]{0,1:T(8,128)} async-done(((f32[4096,1024]{0,1:T(8,128)}), f32[512,1024]{0,1:T(8,128)}) %reduce-scatter.2.cloned.1.call-update) | async-done | bytes 2097168 | tf_op jit(solution)/shard_map/reduce_scatter | solution.py:42
  660.8 150.6 %all-reduce.6.cloned.1.call-done = f32[4,256,256]{1,2,0:T(8,128)} async-done(((f32[4,256,256]{1,2,0:T(8,128)}), f32[4,256,256]{1,2,0:T(8,128)}) %all-reduce.6.cloned.1.call-update) | async-done | bytes 1048592 | tf_op jit(solution)/shard_map/psum | solution.py:63
  816.3 47.1 %custom-call.58 = f32[4,128,128]{2,1,0:T(8,128)S(1)} custom-call(f32[4,128,128]{2,1,0:T(8,128)S(1)} %cholesky.403), custom_call_target="Cholesky" | custom-call | tf_op jit(solution)/shard_map/jit(cholesky)/cholesky | solution.py:64
  864.2 40.7 %custom-call.59 = f32[4,1,128,128]{2,3,1,0:T(8,128)} custom-call(f32[4,1,128,128]{3,2,1,0:T(8,128)} %select_bitcast_fusion), custom_call_target="InvertDiagBlocksLowerTriangular" | custom-call | tf_op jit(solution)/shard_map/jit(cholesky)/cholesky | solution.py:64
  908.7 48.4 %custom-call.60 = f32[4,128,128]{2,1,0:T(8,128)} custom-call(f32[4,128,128]{2,1,0:T(8,128)} %convolution_subtract_fusion.4), custom_call_target="Cholesky" | custom-call | tf_op jit(solution)/shard_map/jit(cholesky)/cholesky | solution.py:64
  961.6 5.3 while.3
  966.9 80.3 %custom-call.61 = f32[4,2,128,128]{2,3,1,0:T(8,128)} custom-call(f32[4,2,128,128]{3,2,1,0:T(8,128)} %bitcast.126), custom_call_target="InvertDiagBlocksLowerTriangular" | custom-call | tf_op jit(solution)/shard_map/triangular_solve | solution.py:66
  1050.1 3.3 fusion.34
  (115 shorter events, 71.7 us)
Async XLA Ops:
  7.2 439.9 %all-reduce.8.cloned.1.call-start = ((), (), s32[]{:S(2)}) async-start(), calls=%async_computation.3 | async-start | bytes 4194304 | tf_op jit(solution)/shard_map/psum | solution.py:12
  20.5 3.0 copy-start
  25.6 1.3 copy-start.1
  50.4 21.5 %copy-start.5 = (f32[2,128,128]{2,1,0:T(8,128)}, f32[2,128,128]{2,1,0:T(8,128)S(1)}, u32[]{:S(2)}) copy-start(f32[2,128,128]{2,1,0:T(8,128)S(1)} %custom-call.50) | copy-start | bytes 393220
  123.2 76.4 %copy-start.6 = (f32[2,128,128]{2,1,0:T(8,128)S(1)}, f32[2,128,128]{2,1,0:T(8,128)}, u32[]{:S(2)}) copy-start(f32[2,128,128]{2,1,0:T(8,128)} %copy-done.5) | copy-start | bytes 393220
  201.0 2.7 copy-start.11
  302.3 2.8 copy-start.10
  319.5 336.0 %reduce-scatter.2.cloned.1.call-start = ((), (), s32[]{:S(2)}) async-start(), calls=%async_computation.1 | async-start | bytes 18874368 | tf_op jit(solution)/shard_map/reduce_scatter | solution.py:42
  462.3 2.6 copy-start.9
  462.3 349.0 %all-reduce.6.cloned.1.call-start = ((), (), s32[]{:S(2)}) async-start(), calls=%async_computation.2 | async-start | bytes 2097152 | tf_op jit(solution)/shard_map/psum | solution.py:63
  811.3 2.6 copy-start.2
  815.3 1.0 copy-start.4
  908.7 52.8 %copy-start.12 = (s32[2]{0:T(128)S(1)}, s32[2]{0:T(128)}, u32[]{:S(2)}) copy-start(s32[2]{0:T(128)} %iota_multiply_fusion) | copy-start | bytes 28
  958.1 1.0 copy-start.3
  961.6 87.3 %copy-start.8 = (f32[128,256]{1,0:T(8,128)S(1)}, f32[128,256]{1,0:T(8,128)}, u32[]{:S(2)}) copy-start(f32[128,256]{1,0:T(8,128)} %get-tuple-element.66) | copy-start | bytes 393220
  1047.2 2.2 copy-start.7
Sparse Core Ops, SparseCore 0:
  319.7 127.3 all-reduce.7
  462.4 193.0 reduce-scatter.1
  660.9 150.3 all-reduce.5
where the time goes:
time: 1070 us; the launch traced here: 1060 us
  other arithmetic  480 us (45%)
  waiting for transfers between devices  468 us (44%)
  matrix products  52.6 us (5%)
  local copies, waits for them, and re-layouts  35.6 us (3%)
  between operations  26.9 us (3%)
    reduce_scatter x1, waiting for transfers between devices, on_device(): lax.psum_scatter(lax.dot_general(solved, panels, (((0, 1), (0, 1)), ((),...  190 us
    another operation x15, other arithmetic, on_device(): lower_factor = jnp.linalg.cholesky(blocks)  164 us
    psum x1, waiting for transfers between devices, on_device(): diag_block = lax.psum(jnp.stack(tiles), ('scen', 'border'))  151 us
    another operation x9, other arithmetic, on_device(): factor = jnp.linalg.cholesky(diag_block)  139 us
    psum x1, waiting for transfers between devices, broadcast(): return lax.psum(kept, axis)  128 us
    another operation x4, other arithmetic, on_device(): lax.linalg.triangular_solve(factor, eye_stack, left_side=True, lower=True)  84 us
    another operation x4, other arithmetic, on_device(): lax.linalg.triangular_solve(lower_factor, identity, left_side=True, lower...  83.4 us
  transfers between devices with their start and end apart: 3, of which 3 were waited for; matrix products, arithmetic and copies ran while one was open for 0% of the time, Pallas kernels for 0%

commit v1 on v0

--- a/solution.py
+++ b/solution.py
@@ -60,7 +60,7 @@
         safe_start = jnp.clip(local_start, 0, share - PW)
         tile = lax.dynamic_slice(schur_cols, (safe_start, jnp.int32(position * PW)), (PW, PW))
         tiles.append(jnp.where(holds, tile, jnp.zeros_like(tile)))
-    diag_block = lax.psum(jnp.stack(tiles), ("scen", "border"))
+    diag_block = lax.psum(lax.psum(jnp.stack(tiles), "border"), "scen")
     factor = jnp.linalg.cholesky(diag_block)
     eye_stack = jnp.broadcast_to(jnp.eye(PW, dtype=jnp.float32), diag_block.shape)
     factor_inverse = lax.linalg.triangular_solve(factor, eye_stack, left_side=True, lower=True)

time: 1070 us -> 1140 us (1.065); the launches traced: 1060 us -> 1120 us
  waiting for transfers between devices: 468 us -> 525 us
    psum x1 -> x2, waiting for transfers between devices: 151 us -> 208 us  [on_device(): diag_block = lax.psum(lax.psum(jnp.stack(tiles), 'border'), 'scen')]
  transfers between devices with their start and end apart: 3 -> 4, of which waited for: 3 -> 4; matrix products, arithmetic and copies ran while one was open for 0% -> 0% of each run, Pallas kernels for 0% -> 0%
where the time goes in v1:
time: 1140 us; the launch traced here: 1120 us
  waiting for transfers between devices  525 us (46%)
  other arithmetic  480 us (42%)
  matrix products  52.6 us (5%)
  local copies, waits for them, and re-layouts  35.7 us (3%)
  between operations  26.9 us (2%)
    psum x2, waiting for transfers between devices, on_device(): diag_block = lax.psum(lax.psum(jnp.stack(tiles), 'border'), 'scen')  208 us
    reduce_scatter x1, waiting for transfers between devices, on_device(): lax.psum_scatter(lax.dot_general(solved, panels, (((0, 1), (0, 1)), ((),...  190 us
    another operation x15, other arithmetic, on_device(): lower_factor = jnp.linalg.cholesky(blocks)  164 us
    another operation x9, other arithmetic, on_device(): factor = jnp.linalg.cholesky(diag_block)  139 us
    psum x1, waiting for transfers between devices, broadcast(): return lax.psum(kept, axis)  128 us
    another operation x4, other arithmetic, on_device(): lax.linalg.triangular_solve(factor, eye_stack, left_side=True, lower=True)  83.9 us
    another operation x4, other arithmetic, on_device(): lax.linalg.triangular_solve(lower_factor, identity, left_side=True, lower...  83.4 us
  transfers between devices with their start and end apart: 4, of which 4 were waited for; matrix products, arithmetic and copies ran while one was open for 0% of the time, Pallas kernels for 0%

profile of v1, /device:TPU:1, one launch (start us, length us, event | category | flops | bytes accessed | tf_op | source)
XLA Modules:
  0.0 1120.2 jit_solution(14440775570741010069)
XLA Ops:
  20.5 3.0 copy.27
  27.0 23.5 %custom-call.50 = f32[2,128,128]{2,1,0:T(8,128)S(1)} custom-call(f32[2,128,128]{2,1,0:T(8,128)S(1)} %cholesky.390), custom_call_target="Cholesky" | custom-call | tf_op jit(solution)/shard_map/jit(cholesky)/cholesky | solution.py:25
  50.5 19.7 %custom-call.51 = f32[2,1,128,128]{2,3,1,0:T(8,128)S(1)} custom-call(f32[2,1,128,128]{3,2,1,0:T(8,128)S(1)} %select_bitcast_fusion.7), custom_call_target="InvertDiagBlocksLowerTriangular" | custom-call | tf_op jit(solution)/shard_map/jit(cholesky)/cholesky | solution.py:25
  74.1 24.9 %custom-call.52 = f32[2,128,128]{2,1,0:T(8,128)} custom-call(f32[2,128,128]{2,1,0:T(8,128)} %cholesky.394), custom_call_target="Cholesky" | custom-call | tf_op jit(solution)/shard_map/jit(cholesky)/cholesky | solution.py:25
  100.6 21.3 %custom-call.53 = f32[2,1,128,128]{2,3,1,0:T(8,128)} custom-call(f32[2,1,128,128]{3,2,1,0:T(8,128)} %get-tuple-element.72), custom_call_target="InvertDiagBlocksLowerTriangular" | custom-call | tf_op jit(solution)/shard_map/jit(cholesky)/cholesky | solution.py:25
  125.4 24.9 %custom-call.54 = f32[2,128,128]{2,1,0:T(8,128)} custom-call(f32[2,128,128]{2,1,0:T(8,128)} %cholesky.399), custom_call_target="Cholesky" | custom-call | tf_op jit(solution)/shard_map/jit(cholesky)/cholesky | solution.py:25
  151.9 21.1 %custom-call.55 = f32[2,1,128,128]{2,3,1,0:T(8,128)} custom-call(f32[2,1,128,128]{3,2,1,0:T(8,128)} %get-tuple-element.70), custom_call_target="InvertDiagBlocksLowerTriangular" | custom-call | tf_op jit(solution)/shard_map/jit(cholesky)/cholesky | solution.py:25
  175.7 23.9 %custom-call.56 = f32[2,128,128]{2,1,0:T(8,128)S(1)} custom-call(f32[2,128,128]{2,1,0:T(8,128)S(1)} %convolution_subtract_fusion.6), custom_call_target="Cholesky" | custom-call | tf_op jit(solution)/shard_map/jit(cholesky)/cholesky | solution.py:25
  203.6 14.1 %while.2 = (s32[]{:T(128)}, f32[2,512,512]{2,1,0:T(8,128)}, s32[4,2]{0,1:T(2,128)S(1)}, f32[4,2,128,128]{3,2,0,1:T(8,128)}, s32[]{:T(128)}) while((s32[]{:T(128)}, f32[2,512,512]{2,1,0:T(8,128)}, s32[4,2]{0,1:T(2,128)S(1)}, f32[4,2,128,128]{3,2,0,1:T(8,128)}, s32[]{:T(128)}) %tuple.68), condition=%wide.while_cond, body=%wide.while_body.sunk | while | flops 2 | bytes 263777 | solution.py:27
  204.2 2.9 bitcast_dynamic-update-slice_fusion.4
  217.7 79.4 %custom-call.57 = f32[2,4,128,128]{2,3,1,0:T(8,128)S(1)} custom-call(f32[2,4,128,128]{3,2,1,0:T(8,128)} %bitcast.125), custom_call_target="InvertDiagBlocksLowerTriangular" | custom-call | tf_op jit(solution)/shard_map/triangular_solve | solution.py:27
  305.3 11.2 fusion.3
  316.5 3.0 dynamic-slice_select_fusion.3
  319.6 127.5 %all-reduce.11.cloned.1.call-done = (bf16[2,512,256]{2,1,0:T(8,128)(2,1)}, bf16[2,512,256]{2,1,0:T(8,128)(2,1)}, bf16[2,512,256]{2,1,0:T(8,128)(2,1)}, bf16[2,512,256]{2,1,0:T(8,128)(2,1)}) async-done(((bf16[2,512,256]{2,1,0:T(8,128)(2,1)}, bf16[2,512,256]{2,1,0:T(8,128)(2,1)}, bf16[2,512,256]{2,1,0:T(8,128)(2,1)}, bf16[2,512,256]{2,1,0:T(8,128)(2,1)}), (bf16[2,512,256]{2,1,0:T(8,128)(2,1)}, ...) | async-done | bytes 2097168 | tf_op jit(solution)/shard_map/psum | solution.py:12
  447.1 15.2 %convolution_bitcast_fusion = f32[4096,1024]{0,1:T(8,128)} fusion(bf16[2,512,4096]{2,1,0:T(8,128)(2,1)} %fusion.3, bf16[2,512,256]{2,1,0:T(8,128)(2,1)} %get-tuple-element.44, bf16[2,512,256]{2,1,0:T(8,128)(2,1)} %get-tuple-element.45, bf16[2,512,256]{2,1,0:T(8,128)(2,1)} %get-tuple-element.46, bf16[2,512,256]{2,1,0:T(8,128)(2,1)} %get-tuple-element.47), kind=kOutput, calls=%fused_computation.4 | convolution fusion | flops 8598323200 | bytes 27262976 | tf_op jit(solution)/shard_map/dot_general | solution.py:43
  465.7 189.9 %reduce-scatter.2.cloned.1.call-done = f32[512,1024]{0,1:T(8,128)} async-done(((f32[4096,1024]{0,1:T(8,128)}), f32[512,1024]{0,1:T(8,128)}) %reduce-scatter.2.cloned.1.call-update) | async-done | bytes 2097168 | tf_op jit(solution)/shard_map/reduce_scatter | solution.py:42
  658.9 122.8 %all-reduce.7.cloned.1.call-done = f32[4,256,256]{1,2,0:T(8,128)} async-done(((f32[4,256,256]{1,2,0:T(8,128)}), f32[4,256,256]{1,2,0:T(8,128)}) %all-reduce.7.cloned.1.call-update) | async-done | bytes 1048592 | tf_op jit(solution)/shard_map/psum | solution.py:63
  783.6 84.8 %all-reduce.9.cloned.1.call-done = f32[4,256,256]{1,2,0:T(8,128)} async-done(((f32[4,256,256]{1,2,0:T(8,128)}), f32[4,256,256]{1,2,0:T(8,128)}) %all-reduce.9.cloned.1.call-update) | async-done | bytes 1048592 | tf_op jit(solution)/shard_map/psum | solution.py:63
  873.4 47.1 %custom-call.58 = f32[4,128,128]{2,1,0:T(8,128)S(1)} custom-call(f32[4,128,128]{2,1,0:T(8,128)S(1)} %cholesky.403), custom_call_target="Cholesky" | custom-call | tf_op jit(solution)/shard_map/jit(cholesky)/cholesky | solution.py:64
  921.3 40.7 %custom-call.59 = f32[4,1,128,128]{2,3,1,0:T(8,128)} custom-call(f32[4,1,128,128]{3,2,1,0:T(8,128)} %select_bitcast_fusion), custom_call_target="InvertDiagBlocksLowerTriangular" | custom-call | tf_op jit(solution)/shard_map/jit(cholesky)/cholesky | solution.py:64
  965.8 48.4 %custom-call.60 = f32[4,128,128]{2,1,0:T(8,128)} custom-call(f32[4,128,128]{2,1,0:T(8,128)} %convolution_subtract_fusion.4), custom_call_target="Cholesky" | custom-call | tf_op jit(solution)/shard_map/jit(cholesky)/cholesky | solution.py:64
  1018.7 5.3 while.3
  1023.9 80.3 %custom-call.61 = f32[4,2,128,128]{2,3,1,0:T(8,128)} custom-call(f32[4,2,128,128]{3,2,1,0:T(8,128)} %bitcast.126), custom_call_target="InvertDiagBlocksLowerTriangular" | custom-call | tf_op jit(solution)/shard_map/triangular_solve | solution.py:66
  1107.1 3.3 fusion.34
  (118 shorter events, 74.6 us)
Async XLA Ops:
  7.2 439.9 %all-reduce.11.cloned.1.call-start = ((), (), s32[]{:S(2)}) async-start(), calls=%async_computation.4 | async-start | bytes 4194304 | tf_op jit(solution)/shard_map/psum | solution.py:12
  20.5 3.0 copy-start
  25.6 1.3 copy-start.1
  50.4 21.5 %copy-start.5 = (f32[2,128,128]{2,1,0:T(8,128)}, f32[2,128,128]{2,1,0:T(8,128)S(1)}, u32[]{:S(2)}) copy-start(f32[2,128,128]{2,1,0:T(8,128)S(1)} %custom-call.50) | copy-start | bytes 393220
  123.2 76.4 %copy-start.6 = (f32[2,128,128]{2,1,0:T(8,128)S(1)}, f32[2,128,128]{2,1,0:T(8,128)}, u32[]{:S(2)}) copy-start(f32[2,128,128]{2,1,0:T(8,128)} %copy-done.5) | copy-start | bytes 393220
  201.0 2.7 copy-start.11
  302.3 2.8 copy-start.10
  319.5 336.0 %reduce-scatter.2.cloned.1.call-start = ((), (), s32[]{:S(2)}) async-start(), calls=%async_computation.1 | async-start | bytes 18874368 | tf_op jit(solution)/shard_map/reduce_scatter | solution.py:42
  462.3 2.6 copy-start.9
  462.3 319.4 %all-reduce.7.cloned.1.call-start = ((), (), s32[]{:S(2)}) async-start(), calls=%async_computation.2 | async-start | bytes 2097152 | tf_op jit(solution)/shard_map/psum | solution.py:63
  658.9 209.5 %all-reduce.9.cloned.1.call-start = ((), (), s32[]{:S(2)}) async-start(), calls=%async_computation.3 | async-start | bytes 2097152 | tf_op jit(solution)/shard_map/psum | solution.py:63
  868.4 2.6 copy-start.2
  872.4 1.0 copy-start.4
  965.8 52.8 %copy-start.12 = (s32[2]{0:T(128)S(1)}, s32[2]{0:T(128)}, u32[]{:S(2)}) copy-start(s32[2]{0:T(128)} %iota_multiply_fusion) | copy-start | bytes 28
  1015.1 1.0 copy-start.3
  1018.6 87.3 %copy-start.8 = (f32[128,256]{1,0:T(8,128)S(1)}, f32[128,256]{1,0:T(8,128)}, u32[]{:S(2)}) copy-start(f32[128,256]{1,0:T(8,128)} %get-tuple-element.66) | copy-start | bytes 393220
  1104.2 2.2 copy-start.7
Sparse Core Ops, SparseCore 0:
  319.7 127.3 all-reduce.10
  462.4 193.0 reduce-scatter.1
  659.0 122.6 all-reduce.6
  784.1 84.2 all-reduce.8
